TPU v7x, 32 devices: a whole 2x2x4 slice. The times are simulated.
32 devices in a mesh: groups: 2 (over y), gx: 4 (over z), gy: 2 (over x), col: 2 (over core).
Axes of the slice: x: 2, y: 2, z: 4, core: 2. Of those that a mesh axis runs over, the one named last changes fastest.
Arguments:
- volume: bfloat16 [32, 16, 2048], P(('groups', 'gx'), ('gy', 'col')), parts along dimension 0, may hold values from -6 to 6
- fine_kernel: bfloat16 [27, 64, 64], replicated, may hold values from -0.15625 to 0.15625
- fine_bias: float32 [64], replicated, may hold values from -3 to 3
- down_kernel: bfloat16 [512, 512], replicated, may hold values from -0.25 to 0.25
- down_bias: float32 [512], replicated, may hold values from -3 to 3
- bottle_kernel: bfloat16 [27, 512, 1024], P(None, None, 'gx'), may hold values from -0.0546875 to 0.0546875
- bottle_bias: float32 [1024], P('gx'), may hold values from -3 to 3
- up_kernel: bfloat16 [1024, 512], replicated, may hold values from -0.1875 to 0.1875
- up_bias: float32 [64], replicated, may hold values from -3 to 3
Outputs:
- decoded: bfloat16 [32, 16, 2048], P(('groups', 'gx'), ('gy', 'col')), parts along dimension 0
There are 2 independent parts, one for each index of `groups`. A program takes and returns all parts, laid end to end along the dimension named above; an argument that names none is the same for every part. Nothing has to cross between parts.
All inputs are finite; a program needn't handle non-finite values.
Results may differ from a plain program's by a relative error of at most 0.0047.
Values may be sent and summed in bfloat16 or wider, within the bound.
A program may use at most 128 MiB of HBM per device.

v0:
```python
import functools

import jax
import jax.numpy as jnp
from jax import lax
from jax.experimental import pallas as pl
from jax.experimental.pallas import tpu as pltpu
from jax.sharding import PartitionSpec as P

MESH = pl.DeviceIdType.MESH
F32 = jnp.float32
BF16 = jnp.bfloat16


def silu(a):
    return (0.5 * a) * (1.0 + jnp.tanh(0.5 * a))


def shifted(a, amount, depth):
    rows = a.shape[0]
    z = lax.broadcasted_iota(jnp.int32, a.shape, 0) % depth
    moved = pltpu.roll(a, amount % rows, 0)
    keep = z >= amount if amount > 0 else z < depth + amount
    return jnp.where(keep, moved, 0.0)


def body(
    sizes,
    vol_hbm,
    fk_hbm,
    fb_ref,
    dk_hbm,
    db_ref,
    bk_hbm,
    bb_ref,
    uk_hbm,
    ub_ref,
    out_ref,
    brick,
    fk,
    band,
    dk,
    bk,
    uk,
    fine_ref,
    strip,
    acc,
    sent,
    back,
    load_sem,
    halo_send,
    halo_recv,
    gather_send,
    gather_recv,
    swap_send,
    swap_recv,
):
    ngx, ngy, ncol = sizes
    nq = ngy * ncol
    cx, cy = out_ref.shape[0], out_ref.shape[1]
    depth, pair = out_ref.shape[2], out_ref.shape[3]
    chans = pair // 2
    hx, hy = cx // 2, cy // 2
    cd = dk.shape[1]
    cb = bk.shape[2]
    g = lax.axis_index("gx")
    q = lax.axis_index("gy") * ncol + lax.axis_index("col")

    def device(gg, qq):
        return {"gx": gg, "gy": qq // ncol, "col": qq % ncol}

    loads = [
        pltpu.make_async_copy(src, dst, load_sem.at[n])
        for n, (src, dst) in enumerate(
            (
                (vol_hbm, brick.at[pl.ds(1, cx), pl.ds(1, cy)]),
                (fk_hbm, fk),
                (dk_hbm, dk),
                (bk_hbm, bk),
                (uk_hbm, uk),
            )
        )
    ]
    for load in loads:
        load.start()

    brick[0] = jnp.zeros_like(brick[0])
    brick[cx + 1] = jnp.zeros_like(brick[0])
    for y in (0, cy + 1):
        brick[1 : cx + 1, y] = jnp.zeros((cx, depth, pair), BF16)
    strip[0] = jnp.zeros_like(strip[0])
    strip[ngx * hx + 1] = jnp.zeros_like(strip[0])

    @pl.when(q == 0)
    def _():
        strip[1 : ngx * hx + 1, 0] = jnp.zeros((ngx * hx, depth, cd), BF16)

    @pl.when(q == nq - 1)
    def _():
        strip[1 : ngx * hx + 1, hy + 1] = jnp.zeros((ngx * hx, depth, cd), BF16)

    barrier = pltpu.get_barrier_semaphore()
    for b in (-1, 0, 1):
        there = jnp.logical_and(q + b >= 0, q + b < nq)

        @pl.when(there)
        def _():
            for d in range(ngx):
                if d or b:
                    pl.semaphore_signal(
                        barrier,
                        inc=1,
                        device_id=device(lax.rem(g + d, ngx), q + b),
                        device_id_type=MESH,
                    )

    inner = jnp.logical_and(q > 0, q < nq - 1)
    pl.semaphore_wait(barrier, jnp.where(inner, 3 * ngx - 1, 2 * ngx - 1))
    loads[0].wait()

    def remote(src, dst, send, recv, gg, qq):
        return pltpu.make_async_remote_copy(
            src_ref=src,
            dst_ref=dst,
            send_sem=send,
            recv_sem=recv,
            device_id=device(gg, qq),
            device_id_type=MESH,
        )

    def edges(step, count):
        if step == 0:
            return pl.ds(1, count), pl.ds(1, count)
        if step > 0:
            return pl.ds(count, 1), pl.ds(0, 1)
        return pl.ds(1, 1), pl.ds(count + 1, 1)

    def valid(gg, qq):
        ok = jnp.logical_and(gg >= 0, gg < ngx)
        return jnp.logical_and(ok, jnp.logical_and(qq >= 0, qq < nq))

    halos = []
    for a in (-1, 0, 1):
        for b in (-1, 0, 1):
            if a == 0 and b == 0:
                continue
            t = len(halos)
            sx, dx = edges(a, cx)
            sy, dy = edges(b, cy)
            halos.append(
                (
                    valid(g + a, q + b),
                    remote(
                        brick.at[sx, sy], brick.at[dx, dy],
                        halo_send.at[t], halo_recv.at[t], g + a, q + b,
                    ),
                    valid(g - a, q - b),
                    remote(
                        brick.at[dx, dy], brick.at[dx, dy],
                        halo_send.at[t], halo_recv.at[t], g - a, q - b,
                    ),
                )
            )
    for ok, out, _, _ in halos:
        pl.when(ok)(out.start)

    loads[1].wait()
    empty = jnp.zeros((chans, chans), BF16)
    for ij in range(9):
        f0, f1, f2 = fk[3 * ij], fk[3 * ij + 1], fk[3 * ij + 2]
        band[ij * pair : ij * pair + chans] = jnp.concatenate([f1, f0, empty, f2], axis=1)
        band[ij * pair + chans : (ij + 1) * pair] = jnp.concatenate([f2, f1, f0, empty], axis=1)

    for _, _, ok, into in halos:
        pl.when(ok)(into.wait_recv)

    pieces = [
        brick[i : i + cx, j : j + cy].reshape(cx * cy * depth, pair)
        for i in range(3)
        for j in range(3)
    ]
    prod = jnp.dot(jnp.concatenate(pieces, axis=1), band[...], preferred_element_type=F32)
    side = prod[:, pair:]
    lane = lax.broadcasted_iota(jnp.int32, side.shape, 1)
    fb = fb_ref[...]
    total = (
        prod[:, :pair]
        + jnp.where(lane < chans, shifted(side, 1, depth), shifted(side, -1, depth))
        + jnp.concatenate([fb, fb], axis=1)
    )
    fine_ref[...] = silu(total).astype(BF16).reshape(cx, cy, depth, pair)

    loads[2].wait()
    cells = []
    for x in range(hx):
        for y in range(hy):
            cells.append(
                jnp.concatenate(
                    [fine_ref[2 * x + dx, 2 * y + dy] for dx in (0, 1) for dy in (0, 1)], axis=1
                )
            )
    coarse = jnp.dot(jnp.concatenate(cells, axis=0), dk[...], preferred_element_type=F32)
    coarse = silu(coarse + db_ref[...]).astype(BF16)
    strip[pl.ds(1 + hx * g, hx), 1 : hy + 1] = coarse.reshape(hx, hy, depth, cd)

    gathers = []
    for d in range(ngx - 1, -1, -1):
        to, source = lax.rem(g + d, ngx), lax.rem(g - d + ngx, ngx)
        for b in (0, -1, 1):
            if d == 0 and b == 0:
                continue
            sy, dy = edges(b, hy)
            s = gather_send.at[d, b + 1]
            r = gather_recv.at[d, b + 1]
            mine, theirs = pl.ds(1 + hx * g, hx), pl.ds(1 + hx * source, hx)
            gathers.append(
                (
                    valid(g, q + b),
                    remote(strip.at[mine, sy], strip.at[mine, dy], s, r, to, q + b),
                    valid(g, q - b),
                    remote(strip.at[theirs, dy], strip.at[theirs, dy], s, r, source, q - b),
                )
            )
    for ok, out, _, _ in gathers:
        pl.when(ok)(out.start)
    loads[3].wait()
    loads[4].wait()
    for _, _, ok, into in gathers:
        pl.when(ok)(into.wait_recv)

    rows = ngx * hx * hy * depth
    acc[...] = jnp.zeros_like(acc)

    @pl.loop(0, 9)
    def _(ij):
        i, j = ij // 3, ij % 3
        lhs = strip[pl.ds(i, ngx * hx), pl.ds(j, hy)].reshape(rows, cd)
        for k in range(3):
            acc[k] += jnp.dot(lhs, bk[3 * ij + k], preferred_element_type=F32)

    bottle = acc[1] + shifted(acc[0], 1, depth) + shifted(acc[2], -1, depth)
    bottle = silu(bottle + bb_ref[...]).astype(BF16)
    sent[...] = bottle.reshape(ngx, hx * hy * depth, cb)
    back[g] = sent[g]

    swaps = []
    for d in range(ngx - 1, 0, -1):
        to, source = lax.rem(g + d, ngx), lax.rem(g - d + ngx, ngx)
        swaps.append(
            (
                remote(sent.at[to], back.at[g], swap_send.at[d], swap_recv.at[d], to, q),
                remote(sent.at[to], back.at[source], swap_send.at[d], swap_recv.at[d], source, q),
            )
        )
    for out, _ in swaps:
        out.start()
    for _, into in swaps:
        into.wait_recv()

    lifted = jnp.zeros((hx * hy * depth, uk.shape[1]), F32)
    for p in range(ngx):
        lifted += jnp.dot(back[p], uk[p * cb : (p + 1) * cb], preferred_element_type=F32)
    ub = ub_ref[...]
    ub = jnp.concatenate([ub, ub], axis=1)
    for x in range(hx):
        for y in range(hy):
            at = (x * hy + y) * depth
            for dx in (0, 1):
                for dy in (0, 1):
                    c = (2 * dx + dy) * pair
                    out_ref[2 * x + dx, 2 * y + dy] = (
                        fine_ref[2 * x + dx, 2 * y + dy].astype(F32)
                        + (lifted[at : at + depth, c : c + pair] + ub)
                    ).astype(BF16)

    for ok, out, _, _ in halos:
        pl.when(ok)(out.wait_send)
    for ok, out, _, _ in gathers:
        pl.when(ok)(out.wait_send)
    for out, _ in swaps:
        out.wait_send()


def local(
    sizes,
    volume,
    fine_kernel,
    fine_bias,
    down_kernel,
    down_bias,
    bottle_kernel,
    bottle_bias,
    up_kernel,
    up_bias,
):
    ngx = sizes[0]
    cx, cy, merged = volume.shape
    chans = fine_kernel.shape[1]
    pair = 2 * chans
    depth = merged // pair
    hx, hy = cx // 2, cy // 2
    cd = down_kernel.shape[1]
    cb = bottle_kernel.shape[2]
    cells = hx * hy * depth
    hbm = pl.BlockSpec(memory_space=pl.ANY)
    vmem = pl.BlockSpec(memory_space=pltpu.VMEM)
    dma = pltpu.SemaphoreType.DMA
    out = pl.pallas_call(
        functools.partial(body, sizes),
        out_shape=jax.ShapeDtypeStruct((cx, cy, depth, pair), BF16),
        in_specs=[hbm, hbm, vmem, hbm, vmem, hbm, vmem, hbm, vmem],
        out_specs=vmem,
        scratch_shapes=[
            pltpu.VMEM((cx + 2, cy + 2, depth, pair), BF16),
            pltpu.VMEM(fine_kernel.shape, BF16),
            pltpu.VMEM((9 * pair, 2 * pair), BF16),
            pltpu.VMEM(down_kernel.shape, BF16),
            pltpu.VMEM(bottle_kernel.shape, BF16),
            pltpu.VMEM(up_kernel.shape, BF16),
            pltpu.VMEM((cx, cy, depth, pair), BF16),
            pltpu.VMEM((ngx * hx + 2, hy + 2, depth, cd), BF16),
            pltpu.VMEM((3, ngx * cells, cb), F32),
            pltpu.VMEM((ngx, cells, cb), BF16),
            pltpu.VMEM((ngx, cells, cb), BF16),
            dma((5,)),
            dma((8,)),
            dma((8,)),
            dma((ngx, 3)),
            dma((ngx, 3)),
            dma((ngx,)),
            dma((ngx,)),
        ],
        compiler_params=pltpu.CompilerParams(
            collective_id=0, has_side_effects=True, vmem_limit_bytes=48 << 20
        ),
    )(
        volume.reshape(cx, cy, depth, pair),
        fine_kernel,
        fine_bias.reshape(1, -1),
        down_kernel,
        down_bias.reshape(1, -1),
        bottle_kernel,
        bottle_bias.reshape(1, -1),
        up_kernel,
        up_bias.reshape(1, -1),
    )
    return out.reshape(cx, cy, merged)


def solution(mesh):
    placed = (
        P(("groups", "gx"), ("gy", "col"), None),
        P(),
        P(),
        P(),
        P(),
        P(None, None, "gx"),
        P("gx"),
        P(),
        P(),
    )
    sizes = tuple(mesh.shape[name] for name in ("gx", "gy", "col"))
    return jax.shard_map(
        functools.partial(local, sizes),
        mesh=mesh,
        in_specs=placed,
        out_specs=P(("groups", "gx"), ("gy", "col"), None),
        check_vma=False,
    )
```

profile of v0, /device:TPU:1, one launch (start us, length us, event | category | flops | bytes accessed | tf_op | source)
XLA Modules:
  0.0 37.1 jit_solution(11753697955259256248)
XLA Ops:
  0.0 0.9 %reshape.18.vol_hbm = bf16[4,4,16,128]{3,2,1,0:T(8,128)(2,1)S(1)} reshape(bf16[4,4,2048]{2,1,0:T(4,128)(2,1)} %param.9) | data formatting | bytes 131072 | tf_op jit(solution)/shard_map/reshape | solution.py:337
  0.9 0.0 copy-start
  0.9 1.2 %copy-done = bf16[1024,512]{1,0:T(8,128)(2,1)S(1)} copy-done((bf16[1024,512]{1,0:T(8,128)(2,1)S(1)}, bf16[1024,512]{1,0:T(8,128)(2,1)}, u32[]{:S(2)}) %copy-start) | copy-done | bytes 1048600
  2.1 0.0 copy-start.1
  2.1 1.0 %copy-done.1 = bf16[512,512]{1,0:T(8,128)(2,1)S(1)} copy-done((bf16[512,512]{1,0:T(8,128)(2,1)S(1)}, bf16[512,512]{1,0:T(8,128)(2,1)}, u32[]{:S(2)}) %copy-start.1) | copy-done | bytes 524312
  3.2 0.0 copy-start.2
  3.2 1.0 %copy-done.2 = bf16[27,64,64]{2,1,0:T(8,128)(2,1)S(1)} copy-done((bf16[27,64,64]{2,1,0:T(8,128)(2,1)S(1)}, bf16[27,64,64]{2,1,0:T(8,128)(2,1)}, u32[]{:S(2)}) %copy-start.2) | copy-done | bytes 221208
  4.2 0.0 copy-start.3
  4.2 0.7 %copy-done.3 = f32[512]{0:T(512)S(1)} copy-done((f32[512]{0:T(512)S(1)}, f32[512]{0:T(512)}, u32[]{:S(2)}) %copy-start.3) | copy-done | bytes 2072
  4.9 0.0 copy-start.4
  4.9 0.7 %copy-done.4 = f32[256]{0:T(256)S(1)} copy-done((f32[256]{0:T(256)S(1)}, f32[256]{0:T(256)}, u32[]{:S(2)}) %copy-start.4) | copy-done | bytes 1048
  5.5 0.0 copy-start.5
  5.5 0.7 %copy-done.5 = f32[64]{0:T(128)S(1)} copy-done((f32[64]{0:T(128)S(1)}, f32[64]{0:T(128)}, u32[]{:S(2)}) %copy-start.5) | copy-done | bytes 280
  6.2 0.0 copy-start.6
  6.2 0.7 %copy-done.6 = f32[64]{0:T(128)S(1)} copy-done((f32[64]{0:T(128)S(1)}, f32[64]{0:T(128)}, u32[]{:S(2)}) %copy-start.6) | copy-done | bytes 280
  6.8 29.6 %shard_map.91 = bf16[4,4,16,128]{3,2,1,0:T(8,128)(2,1)S(1)} custom-call(bf16[4,4,16,128]{3,2,1,0:T(8,128)(2,1)S(1)} %reshape.18.vol_hbm, bf16[27,64,64]{2,1,0:T(8,128)(2,1)S(1)} %copy-done.2, f32[1,64]{1,0:T(1,128)S(1)} %bitcast.8, bf16[512,512]{1,0:T(8,128)(2,1)S(1)} %copy-done.1, f32[1,512]{1,0:T(1,128)S(1)} %bitcast.6, bf16[27,512,256]{2,1,0:T(8,128)(2,1)} %bk_hbm.1, ...), custom_call_target="tpu_custom_call" | custom-call | tf_op jit(solution)/shard_map/pallas_call | solution.py:308
  36.5 0.6 %reshape.23 = bf16[4,4,2048]{2,1,0:T(4,128)(2,1)} reshape(bf16[4,4,16,128]{3,2,1,0:T(8,128)(2,1)S(1)} %shard_map.91) | data formatting | bytes 131072 | tf_op jit(solution)/shard_map/reshape | solution.py:347
Async XLA Ops:
  0.9 1.2 %copy-start = (bf16[1024,512]{1,0:T(8,128)(2,1)S(1)}, bf16[1024,512]{1,0:T(8,128)(2,1)}, u32[]{:S(2)}) copy-start(bf16[1024,512]{1,0:T(8,128)(2,1)} %uk_hbm.1) | copy-start | bytes 3145732
  2.1 1.0 %copy-start.1 = (bf16[512,512]{1,0:T(8,128)(2,1)S(1)}, bf16[512,512]{1,0:T(8,128)(2,1)}, u32[]{:S(2)}) copy-start(bf16[512,512]{1,0:T(8,128)(2,1)} %dk_hbm.1) | copy-start | bytes 1572868
  3.2 1.0 %copy-start.2 = (bf16[27,64,64]{2,1,0:T(8,128)(2,1)S(1)}, bf16[27,64,64]{2,1,0:T(8,128)(2,1)}, u32[]{:S(2)}) copy-start(bf16[27,64,64]{2,1,0:T(8,128)(2,1)} %fk_hbm.1) | copy-start | bytes 663556
  4.2 0.7 %copy-start.3 = (f32[512]{0:T(512)S(1)}, f32[512]{0:T(512)}, u32[]{:S(2)}) copy-start(f32[512]{0:T(512)} %param.13) | copy-start | bytes 6148
  4.9 0.7 %copy-start.4 = (f32[256]{0:T(256)S(1)}, f32[256]{0:T(256)}, u32[]{:S(2)}) copy-start(f32[256]{0:T(256)} %param.15) | copy-start | bytes 3076
  5.5 0.7 %copy-start.5 = (f32[64]{0:T(128)S(1)}, f32[64]{0:T(128)}, u32[]{:S(2)}) copy-start(f32[64]{0:T(128)} %param.11) | copy-start | bytes 772
  6.2 0.7 %copy-start.6 = (f32[64]{0:T(128)S(1)}, f32[64]{0:T(128)}, u32[]{:S(2)}) copy-start(f32[64]{0:T(128)} %param.17) | copy-start | bytes 772
where the time goes:
time: 37.9 us; the launch traced here: 37.1 us
  Pallas kernels  29.6 us (78%)
  local copies, waits for them, and re-layouts  7.48 us (20%)
    pallas_call x1, Pallas kernels, local(): pl.pallas_call(functools.partial(body, sizes), out_shape=jax.ShapeDtypeSt...  29.6 us
    unnamed x14, local copies, waits for them, and re-layouts  5.94 us
    reshape x1, local copies, waits for them, and re-layouts, local(): volume.reshape(cx, cy, depth, pair)  0.88 us

commit v1 on v0

--- a/solution.py
+++ b/solution.py
@@ -28,13 +28,13 @@
     sizes,
     vol_hbm,
     fk_hbm,
-    fb_ref,
+    fb_hbm,
     dk_hbm,
-    db_ref,
+    db_hbm,
     bk_hbm,
-    bb_ref,
+    bb_hbm,
     uk_hbm,
-    ub_ref,
+    ub_hbm,
     out_ref,
     brick,
     fk,
@@ -42,6 +42,10 @@
     dk,
     bk,
     uk,
+    fb_ref,
+    db_ref,
+    bb_ref,
+    ub_ref,
     fine_ref,
     strip,
     acc,
@@ -75,10 +79,14 @@
             (
                 (vol_hbm, brick.at[pl.ds(1, cx), pl.ds(1, cy)]),
                 (fk_hbm, fk),
+                (fb_hbm, fb_ref),
                 (dk_hbm, dk),
-                (bk_hbm, bk),
+                (db_hbm, db_ref),
+                (bb_hbm, bb_ref),
                 (uk_hbm, uk),
-            )
+                (ub_hbm, ub_ref),
+            )
+            + tuple((bk_hbm.at[pl.ds(3 * n, 3)], bk.at[pl.ds(3 * n, 3)]) for n in range(9))
         )
     ]
     for load in loads:
@@ -179,6 +187,7 @@
         for i in range(3)
         for j in range(3)
     ]
+    loads[2].wait()
     prod = jnp.dot(jnp.concatenate(pieces, axis=1), band[...], preferred_element_type=F32)
     side = prod[:, pair:]
     lane = lax.broadcasted_iota(jnp.int32, side.shape, 1)
@@ -190,7 +199,8 @@
     )
     fine_ref[...] = silu(total).astype(BF16).reshape(cx, cy, depth, pair)
 
-    loads[2].wait()
+    loads[3].wait()
+    loads[4].wait()
     cells = []
     for x in range(hx):
         for y in range(hy):
@@ -223,8 +233,8 @@
             )
     for ok, out, _, _ in gathers:
         pl.when(ok)(out.start)
-    loads[3].wait()
-    loads[4].wait()
+    for load in loads[5:]:
+        load.wait()
     for _, _, ok, into in gathers:
         pl.when(ok)(into.wait_recv)
 
@@ -302,13 +312,13 @@
     cd = down_kernel.shape[1]
     cb = bottle_kernel.shape[2]
     cells = hx * hy * depth
-    hbm = pl.BlockSpec(memory_space=pl.ANY)
+    hbm = pl.BlockSpec(memory_space=pltpu.HBM)
     vmem = pl.BlockSpec(memory_space=pltpu.VMEM)
     dma = pltpu.SemaphoreType.DMA
     out = pl.pallas_call(
         functools.partial(body, sizes),
         out_shape=jax.ShapeDtypeStruct((cx, cy, depth, pair), BF16),
-        in_specs=[hbm, hbm, vmem, hbm, vmem, hbm, vmem, hbm, vmem],
+        in_specs=[hbm] * 9,
         out_specs=vmem,
         scratch_shapes=[
             pltpu.VMEM((cx + 2, cy + 2, depth, pair), BF16),
@@ -317,12 +327,16 @@
             pltpu.VMEM(down_kernel.shape, BF16),
             pltpu.VMEM(bottle_kernel.shape, BF16),
             pltpu.VMEM(up_kernel.shape, BF16),
+            pltpu.VMEM((1, chans), F32),
+            pltpu.VMEM((1, cd), F32),
+            pltpu.VMEM((1, cb), F32),
+            pltpu.VMEM((1, chans), F32),
             pltpu.VMEM((cx, cy, depth, pair), BF16),
             pltpu.VMEM((ngx * hx + 2, hy + 2, depth, cd), BF16),
             pltpu.VMEM((3, ngx * cells, cb), F32),
             pltpu.VMEM((ngx, cells, cb), BF16),
             pltpu.VMEM((ngx, cells, cb), BF16),
-            dma((5,)),
+            dma((17,)),
             dma((8,)),
             dma((8,)),
             dma((ngx, 3)),
@@ -331,7 +345,7 @@
             dma((ngx,)),
         ],
         compiler_params=pltpu.CompilerParams(
-            collective_id=0, has_side_effects=True, vmem_limit_bytes=48 << 20
+            collective_id=0, has_side_effects=True, vmem_limit_bytes=60 << 20
         ),
     )(
         volume.reshape(cx, cy, depth, pair),

time: 37.9 us -> 33.6 us (0.89)
  local copies, waits for them, and re-layouts: 7.48 us -> 3 us
  Pallas kernels: 29.6 us -> 30.1 us
    unnamed x14 -> x0, local copies, waits for them, and re-layouts: 5.94 us -> none
    reshape x1, local copies, waits for them, and re-layouts: 0.65 us -> 1.49 us  [local(): return out.reshape(cx, cy, merged)]
    reshape x1, local copies, waits for them, and re-layouts: 0.88 us -> 1.51 us  [local(): volume.reshape(cx, cy, depth, pair)]
    pallas_call x1, Pallas kernels: 29.6 us -> 30.1 us  [local(): pl.pallas_call(functools.partial(body, sizes), out_shape=jax.ShapeDtypeSt...]
where the time goes in v1:
time: 33.6 us; the launch traced here: 33.1 us
  Pallas kernels  30.1 us (90%)
  local copies, waits for them, and re-layouts  3 us (9%)
    pallas_call x1, Pallas kernels, local(): pl.pallas_call(functools.partial(body, sizes), out_shape=jax.ShapeDtypeSt...  30.1 us
    reshape x1, local copies, waits for them, and re-layouts, local(): volume.reshape(cx, cy, depth, pair)  1.51 us
    reshape x1, local copies, waits for them, and re-layouts, local(): return out.reshape(cx, cy, merged)  1.49 us

profile of v1, /device:TPU:1, one launch (start us, length us, event | category | flops | bytes accessed | tf_op | source)
XLA Modules:
  0.0 33.1 jit_solution(181941724546715297)
XLA Ops:
  0.0 1.5 %reshape.18.vol_hbm = bf16[4,4,16,128]{3,2,1,0:T(8,128)(2,1)} reshape(bf16[4,4,2048]{2,1,0:T(4,128)(2,1)} %param.9) | data formatting | bytes 131072 | tf_op jit(solution)/shard_map/reshape | solution.py:351
  1.5 30.1 %shard_map.91 = bf16[4,4,16,128]{3,2,1,0:T(8,128)(2,1)} custom-call(bf16[4,4,16,128]{3,2,1,0:T(8,128)(2,1)} %reshape.18.vol_hbm, bf16[27,64,64]{2,1,0:T(8,128)(2,1)} %fk_hbm.1, f32[1,64]{1,0:T(1,128)} %bitcast.8, bf16[512,512]{1,0:T(8,128)(2,1)} %dk_hbm.1, f32[1,512]{1,0:T(1,128)} %bitcast.6, bf16[27,512,256]{2,1,0:T(8,128)(2,1)} %bk_hbm.1, ...), custom_call_target="tpu_custom_call" | custom-call | tf_op jit(solution)/shard_map/pallas_call | solution.py:318
  31.6 1.5 %reshape.23 = bf16[4,4,2048]{2,1,0:T(4,128)(2,1)} reshape(bf16[4,4,16,128]{3,2,1,0:T(8,128)(2,1)} %shard_map.91) | data formatting | bytes 131072 | tf_op jit(solution)/shard_map/reshape | solution.py:361

commit v2 on v1

--- a/solution.py
+++ b/solution.py
@@ -36,6 +36,7 @@
     uk_hbm,
     ub_hbm,
     out_ref,
+    raw,
     brick,
     fk,
     band,
@@ -56,6 +57,8 @@
     halo_recv,
     gather_send,
     gather_recv,
+    rim_send,
+    rim_recv,
     swap_send,
     swap_recv,
 ):
@@ -77,7 +80,7 @@
         pltpu.make_async_copy(src, dst, load_sem.at[n])
         for n, (src, dst) in enumerate(
             (
-                (vol_hbm, brick.at[pl.ds(1, cx), pl.ds(1, cy)]),
+                (vol_hbm, raw),
                 (fk_hbm, fk),
                 (fb_hbm, fb_ref),
                 (dk_hbm, dk),
@@ -107,24 +110,30 @@
     def _():
         strip[1 : ngx * hx + 1, hy + 1] = jnp.zeros((ngx * hx, depth, cd), BF16)
 
+    def valid(gg, qq):
+        ok = jnp.logical_and(gg >= 0, gg < ngx)
+        return jnp.logical_and(ok, jnp.logical_and(qq >= 0, qq < nq))
+
     barrier = pltpu.get_barrier_semaphore()
-    for b in (-1, 0, 1):
-        there = jnp.logical_and(q + b >= 0, q + b < nq)
-
-        @pl.when(there)
-        def _():
-            for d in range(ngx):
-                if d or b:
-                    pl.semaphore_signal(
-                        barrier,
-                        inc=1,
-                        device_id=device(lax.rem(g + d, ngx), q + b),
-                        device_id_type=MESH,
-                    )
-
-    inner = jnp.logical_and(q > 0, q < nq - 1)
-    pl.semaphore_wait(barrier, jnp.where(inner, 3 * ngx - 1, 2 * ngx - 1))
+
+    def greet(gg, qq):
+        pl.semaphore_signal(barrier, inc=1, device_id=device(gg, qq), device_id_type=MESH)
+
+    partners = ngx - 1
+    for b in (-1, 1):
+        for a in (-1, 0, 1):
+            there = valid(g + a, q + b)
+            pl.when(there)(functools.partial(greet, g + a, q + b))
+            partners += there.astype(jnp.int32)
+    for d in range(1, ngx):
+        greet(lax.rem(g + d, ngx), q)
+
     loads[0].wait()
+    for x in range(cx):
+        brick[1 + x, 1 : cy + 1] = (
+            raw[x].astype(F32).reshape(cy, depth, pair).astype(BF16)
+        )
+    pl.semaphore_wait(barrier, partners)
 
     def remote(src, dst, send, recv, gg, qq):
         return pltpu.make_async_remote_copy(
@@ -142,10 +151,6 @@
         if step > 0:
             return pl.ds(count, 1), pl.ds(0, 1)
         return pl.ds(1, 1), pl.ds(count + 1, 1)
-
-    def valid(gg, qq):
-        ok = jnp.logical_and(gg >= 0, gg < ngx)
-        return jnp.logical_and(ok, jnp.logical_and(qq >= 0, qq < nq))
 
     halos = []
     for a in (-1, 0, 1):
@@ -213,63 +218,89 @@
     coarse = silu(coarse + db_ref[...]).astype(BF16)
     strip[pl.ds(1 + hx * g, hx), 1 : hy + 1] = coarse.reshape(hx, hy, depth, cd)
 
-    gathers = []
-    for d in range(ngx - 1, -1, -1):
-        to, source = lax.rem(g + d, ngx), lax.rem(g - d + ngx, ngx)
-        for b in (0, -1, 1):
-            if d == 0 and b == 0:
-                continue
-            sy, dy = edges(b, hy)
-            s = gather_send.at[d, b + 1]
-            r = gather_recv.at[d, b + 1]
-            mine, theirs = pl.ds(1 + hx * g, hx), pl.ds(1 + hx * source, hx)
-            gathers.append(
-                (
-                    valid(g, q + b),
-                    remote(strip.at[mine, sy], strip.at[mine, dy], s, r, to, q + b),
-                    valid(g, q - b),
-                    remote(strip.at[theirs, dy], strip.at[theirs, dy], s, r, source, q - b),
-                )
-            )
-    for ok, out, _, _ in gathers:
-        pl.when(ok)(out.start)
+    def planes(at):
+        return pl.ds(1 + hx * at, hx)
+
+    def block(source, to):
+        ref = strip.at[planes(source), pl.ds(1, hy)]
+        return remote(ref, ref, gather_send.at[to], gather_recv.at[source], to, q)
+
+    def rim(at, b, sending):
+        sy, dy = edges(b, hy)
+        dst = strip.at[planes(at), dy]
+        src = strip.at[planes(at), sy] if sending else dst
+        t = (b + 1) // 2
+        beside = q + b if sending else q - b
+        return remote(src, dst, rim_send.at[at, t], rim_recv.at[at, t], g, beside)
+
+    def rims(at, sending, action):
+        for b in (-1, 1):
+            other = q + b if sending else q - b
+            pl.when(valid(g, other))(getattr(rim(at, b, sending), action))
+
+    def others(visit):
+        for d in range(1, ngx):
+            for p in (g + d, g - d):
+                pl.when(valid(p, q))(functools.partial(visit, p))
+
+    others(lambda p: block(g, p).start())
+    rims(g, True, "start")
+    acc[...] = jnp.zeros_like(acc)
     for load in loads[5:]:
         load.wait()
-    for _, _, ok, into in gathers:
-        pl.when(ok)(into.wait_recv)
-
-    rows = ngx * hx * hy * depth
-    acc[...] = jnp.zeros_like(acc)
-
-    @pl.loop(0, 9)
-    def _(ij):
-        i, j = ij // 3, ij % 3
-        lhs = strip[pl.ds(i, ngx * hx), pl.ds(j, hy)].reshape(rows, cd)
-        for k in range(3):
-            acc[k] += jnp.dot(lhs, bk[3 * ij + k], preferred_element_type=F32)
-
-    bottle = acc[1] + shifted(acc[0], 1, depth) + shifted(acc[2], -1, depth)
-    bottle = silu(bottle + bb_ref[...]).astype(BF16)
-    sent[...] = bottle.reshape(ngx, hx * hy * depth, cb)
-    back[g] = sent[g]
-
-    swaps = []
+
+    def part(source, columns):
+        lhs = [strip[planes(source), j : j + hy].reshape(hx * hy * depth, cd) for j in columns]
+        for i in range(3):
+            at = pl.ds(2 + hx * source - i, hx)
+            for k in range(3):
+                term = sum(
+                    jnp.dot(piece, bk[9 * i + 3 * j + k], preferred_element_type=F32)
+                    for piece, j in zip(lhs, columns)
+                )
+                acc[k, at] += term.reshape(hx, hy * depth, cb)
+
+    def source_of(n):
+        return g + jnp.where(n % 2 == 1, (n + 1) // 2, -((n + 1) // 2))
+
+    @pl.loop(0, 2 * ngx)
+    def _(n):
+        now, before = source_of(n), source_of(n - 1)
+        ready = jnp.logical_and(valid(now, q), n < 2 * ngx - 1)
+
+        @pl.when(jnp.logical_and(ready, n > 0))
+        def _():
+            block(now, now).wait_recv()
+            rims(now, True, "start")
+
+        @pl.when(jnp.logical_and(valid(before, q), n > 0))
+        def _():
+            rims(before, False, "wait_recv")
+            part(before, (0, 2))
+
+        @pl.when(ready)
+        def _():
+            part(now, (1,))
+
+    def swap(to, source):
+        return remote(sent.at[to], back.at[source], swap_send.at[to], swap_recv.at[source], to, q)
+
+    def finish(p):
+        at = pl.ds(1 + hx * p, hx)
+        taps = [acc[k, at].reshape(hx * hy * depth, cb) for k in range(3)]
+        bottle = taps[1] + shifted(taps[0], 1, depth) + shifted(taps[2], -1, depth)
+        return silu(bottle + bb_ref[...]).astype(BF16)
+
     for d in range(ngx - 1, 0, -1):
-        to, source = lax.rem(g + d, ngx), lax.rem(g - d + ngx, ngx)
-        swaps.append(
-            (
-                remote(sent.at[to], back.at[g], swap_send.at[d], swap_recv.at[d], to, q),
-                remote(sent.at[to], back.at[source], swap_send.at[d], swap_recv.at[d], source, q),
-            )
-        )
-    for out, _ in swaps:
-        out.start()
-    for _, into in swaps:
-        into.wait_recv()
-
-    lifted = jnp.zeros((hx * hy * depth, uk.shape[1]), F32)
-    for p in range(ngx):
-        lifted += jnp.dot(back[p], uk[p * cb : (p + 1) * cb], preferred_element_type=F32)
+        to = lax.rem(g + d, ngx)
+        sent[to] = finish(to)
+        swap(to, g).start()
+
+    lifted = jnp.dot(finish(g), uk[g], preferred_element_type=F32)
+    for d in range(1, ngx):
+        source = lax.rem(g + d, ngx)
+        swap(source, source).wait_recv()
+        lifted += jnp.dot(back[source], uk[source], preferred_element_type=F32)
     ub = ub_ref[...]
     ub = jnp.concatenate([ub, ub], axis=1)
     for x in range(hx):
@@ -285,10 +316,10 @@
 
     for ok, out, _, _ in halos:
         pl.when(ok)(out.wait_send)
-    for ok, out, _, _ in gathers:
-        pl.when(ok)(out.wait_send)
-    for out, _ in swaps:
-        out.wait_send()
+    others(lambda p: block(g, p).wait_send())
+    others(lambda p: swap(p, g).wait_send())
+    for at in range(ngx):
+        rims(at, True, "wait_send")
 
 
 def local(
@@ -321,26 +352,29 @@
         in_specs=[hbm] * 9,
         out_specs=vmem,
         scratch_shapes=[
+            pltpu.VMEM(volume.shape, BF16),
             pltpu.VMEM((cx + 2, cy + 2, depth, pair), BF16),
             pltpu.VMEM(fine_kernel.shape, BF16),
             pltpu.VMEM((9 * pair, 2 * pair), BF16),
             pltpu.VMEM(down_kernel.shape, BF16),
             pltpu.VMEM(bottle_kernel.shape, BF16),
-            pltpu.VMEM(up_kernel.shape, BF16),
+            pltpu.VMEM((ngx, cb, up_kernel.shape[1]), BF16),
             pltpu.VMEM((1, chans), F32),
             pltpu.VMEM((1, cd), F32),
             pltpu.VMEM((1, cb), F32),
             pltpu.VMEM((1, chans), F32),
             pltpu.VMEM((cx, cy, depth, pair), BF16),
             pltpu.VMEM((ngx * hx + 2, hy + 2, depth, cd), BF16),
-            pltpu.VMEM((3, ngx * cells, cb), F32),
+            pltpu.VMEM((3, ngx * hx + 2, hy * depth, cb), F32),
             pltpu.VMEM((ngx, cells, cb), BF16),
             pltpu.VMEM((ngx, cells, cb), BF16),
             dma((17,)),
             dma((8,)),
             dma((8,)),
-            dma((ngx, 3)),
-            dma((ngx, 3)),
+            dma((ngx,)),
+            dma((ngx,)),
+            dma((ngx, 2)),
+            dma((ngx, 2)),
             dma((ngx,)),
             dma((ngx,)),
         ],
@@ -348,14 +382,14 @@
             collective_id=0, has_side_effects=True, vmem_limit_bytes=60 << 20
         ),
     )(
-        volume.reshape(cx, cy, depth, pair),
+        volume,
         fine_kernel,
         fine_bias.reshape(1, -1),
         down_kernel,
         down_bias.reshape(1, -1),
         bottle_kernel,
         bottle_bias.reshape(1, -1),
-        up_kernel,
+        up_kernel.reshape(ngx, cb, -1),
         up_bias.reshape(1, -1),
     )
     return out.reshape(cx, cy, merged)

time: 33.6 us -> 30.6 us (0.911); the launches traced: 33.1 us -> 30.4 us
  local copies, waits for them, and re-layouts: 3 us -> 1.49 us
  Pallas kernels: 30.1 us -> 28.9 us
    reshape x1 -> x0, local copies, waits for them, and re-layouts: 1.51 us -> none  [local(): volume.reshape(cx, cy, depth, pair)]
    pallas_call x1, Pallas kernels: 30.1 us -> 28.9 us  [local(): pl.pallas_call(functools.partial(body, sizes), out_shape=jax.ShapeDtypeSt...]
where the time goes in v2:
time: 30.6 us; the launch traced here: 30.4 us
  Pallas kernels  28.9 us (94%)
  local copies, waits for them, and re-layouts  1.49 us (5%)
    pallas_call x1, Pallas kernels, local(): pl.pallas_call(functools.partial(body, sizes), out_shape=jax.ShapeDtypeSt...  28.9 us
    reshape x1, local copies, waits for them, and re-layouts, local(): return out.reshape(cx, cy, merged)  1.49 us

profile of v2, /device:TPU:1, one launch (start us, length us, event | category | flops | bytes accessed | tf_op | source)
XLA Modules:
  0.0 30.4 jit_solution(13388139081700191910)
XLA Ops:
  0.0 28.9 %shard_map.91 = bf16[4,4,16,128]{3,2,1,0:T(8,128)(2,1)} custom-call(bf16[4,4,2048]{2,1,0:T(4,128)(2,1)} %vol_hbm.1, bf16[27,64,64]{2,1,0:T(8,128)(2,1)} %fk_hbm.1, f32[1,64]{1,0:T(1,128)} %bitcast.10, bf16[512,512]{1,0:T(8,128)(2,1)} %dk_hbm.1, f32[1,512]{1,0:T(1,128)} %bitcast.8, bf16[27,512,256]{2,1,0:T(8,128)(2,1)} %bk_hbm.1, f32[1,256]{1,0:T(1,128)} %bitcast.9, ...), custom_call_target="tpu_custom_call" | custom-call | tf_op jit(solution)/shard_map/pallas_call | solution.py:349
  28.9 1.5 %reshape.23 = bf16[4,4,2048]{2,1,0:T(4,128)(2,1)} reshape(bf16[4,4,16,128]{3,2,1,0:T(8,128)(2,1)} %shard_map.91) | data formatting | bytes 131072 | tf_op jit(solution)/shard_map/reshape | solution.py:395

commit v3 on v2

--- a/solution.py
+++ b/solution.py
@@ -64,8 +64,7 @@
 ):
     ngx, ngy, ncol = sizes
     nq = ngy * ncol
-    cx, cy = out_ref.shape[0], out_ref.shape[1]
-    depth, pair = out_ref.shape[2], out_ref.shape[3]
+    cx, cy, depth, pair = fine_ref.shape
     chans = pair // 2
     hx, hy = cx // 2, cy // 2
     cd = dk.shape[1]
@@ -263,25 +262,6 @@
     def source_of(n):
         return g + jnp.where(n % 2 == 1, (n + 1) // 2, -((n + 1) // 2))
 
-    @pl.loop(0, 2 * ngx)
-    def _(n):
-        now, before = source_of(n), source_of(n - 1)
-        ready = jnp.logical_and(valid(now, q), n < 2 * ngx - 1)
-
-        @pl.when(jnp.logical_and(ready, n > 0))
-        def _():
-            block(now, now).wait_recv()
-            rims(now, True, "start")
-
-        @pl.when(jnp.logical_and(valid(before, q), n > 0))
-        def _():
-            rims(before, False, "wait_recv")
-            part(before, (0, 2))
-
-        @pl.when(ready)
-        def _():
-            part(now, (1,))
-
     def swap(to, source):
         return remote(sent.at[to], back.at[source], swap_send.at[to], swap_recv.at[source], to, q)
 
@@ -291,10 +271,41 @@
         bottle = taps[1] + shifted(taps[0], 1, depth) + shifted(taps[2], -1, depth)
         return silu(bottle + bb_ref[...]).astype(BF16)
 
-    for d in range(ngx - 1, 0, -1):
-        to = lax.rem(g + d, ngx)
-        sent[to] = finish(to)
-        swap(to, g).start()
+    def position(source):
+        ahead = source - g
+        return jnp.where(ahead > 0, 2 * ahead - 1, -2 * ahead)
+
+    def last_step(p):
+        far = position(p)
+        for beside in (p - 1, p + 1):
+            far = jnp.maximum(far, jnp.where(valid(beside, q), position(beside), 0))
+        return far + 1
+
+    @pl.loop(0, 2 * ngx)
+    def _(n):
+        now, before = source_of(n), source_of(n - 1)
+        ready = jnp.logical_and(valid(now, q), n < 2 * ngx - 1)
+
+        @pl.when(jnp.logical_and(ready, n > 0))
+        def _():
+            block(now, now).wait_recv()
+            rims(now, True, "start")
+
+        @pl.when(jnp.logical_and(valid(before, q), n > 0))
+        def _():
+            rims(before, False, "wait_recv")
+            part(before, (0, 2))
+
+        @pl.when(ready)
+        def _():
+            part(now, (1,))
+
+        @pl.loop(0, ngx)
+        def _(p):
+            @pl.when(jnp.logical_and(p != g, last_step(p) == n))
+            def _():
+                sent[p] = finish(p)
+                swap(p, g).start()
 
     lifted = jnp.dot(finish(g), uk[g], preferred_element_type=F32)
     for d in range(1, ngx):
@@ -304,15 +315,18 @@
     ub = ub_ref[...]
     ub = jnp.concatenate([ub, ub], axis=1)
     for x in range(hx):
-        for y in range(hy):
-            at = (x * hy + y) * depth
-            for dx in (0, 1):
+        for dx in (0, 1):
+            columns = []
+            for y in range(hy):
+                at = (x * hy + y) * depth
                 for dy in (0, 1):
                     c = (2 * dx + dy) * pair
-                    out_ref[2 * x + dx, 2 * y + dy] = (
+                    columns.append(
                         fine_ref[2 * x + dx, 2 * y + dy].astype(F32)
                         + (lifted[at : at + depth, c : c + pair] + ub)
-                    ).astype(BF16)
+                    )
+            whole = jnp.stack(columns).reshape(cy, depth * pair)
+            out_ref[2 * x + dx] = whole.astype(BF16)
 
     for ok, out, _, _ in halos:
         pl.when(ok)(out.wait_send)
@@ -346,9 +360,9 @@
     hbm = pl.BlockSpec(memory_space=pltpu.HBM)
     vmem = pl.BlockSpec(memory_space=pltpu.VMEM)
     dma = pltpu.SemaphoreType.DMA
-    out = pl.pallas_call(
+    return pl.pallas_call(
         functools.partial(body, sizes),
-        out_shape=jax.ShapeDtypeStruct((cx, cy, depth, pair), BF16),
+        out_shape=jax.ShapeDtypeStruct((cx, cy, merged), BF16),
         in_specs=[hbm] * 9,
         out_specs=vmem,
         scratch_shapes=[
@@ -392,7 +406,6 @@
         up_kernel.reshape(ngx, cb, -1),
         up_bias.reshape(1, -1),
     )
-    return out.reshape(cx, cy, merged)
 
 
 def solution(mesh):

time: 30.6 us -> 29.9 us (0.977)
  Pallas kernels: 28.9 us -> 28.2 us
    unnamed x0 -> x1, local copies, waits for them, and re-layouts: none -> 1.49 us
    reshape x1 -> x0, local copies, waits for them, and re-layouts: 1.49 us -> none  [local(): return out.reshape(cx, cy, merged)]
    pallas_call x1, Pallas kernels: 28.9 us -> 28.2 us  [local(): pl.pallas_call(functools.partial(body, sizes), out_shape=jax.ShapeDtypeSt...]
where the time goes in v3:
time: 29.9 us; the launch traced here: 29.7 us
  Pallas kernels  28.2 us (94%)
  local copies, waits for them, and re-layouts  1.49 us (5%)
    pallas_call x1, Pallas kernels, local(): pl.pallas_call(functools.partial(body, sizes), out_shape=jax.ShapeDtypeSt...  28.2 us
    unnamed x1, local copies, waits for them, and re-layouts  1.49 us

profile of v3, /device:TPU:1, one launch (start us, length us, event | category | flops | bytes accessed | tf_op | source)
XLA Modules:
  0.0 29.7 jit_solution(17528380790881976517)
XLA Ops:
  0.0 28.2 %shard_map.91 = bf16[4,4,2048]{2,1,0:T(4,128)(2,1)} custom-call(bf16[4,4,2048]{2,1,0:T(4,128)(2,1)} %vol_hbm.1, bf16[27,64,64]{2,1,0:T(8,128)(2,1)} %fk_hbm.1, f32[1,64]{1,0:T(1,128)} %bitcast.8, bf16[512,512]{1,0:T(8,128)(2,1)} %dk_hbm.1, f32[1,512]{1,0:T(1,128)} %bitcast.6, bf16[27,512,256]{2,1,0:T(8,128)(2,1)} %bk_hbm.1, f32[1,256]{1,0:T(1,128)} %bitcast.7, ...), custom_call_target="tpu_custom_call" | custom-call | tf_op jit(solution)/shard_map/pallas_call | solution.py:363
  28.2 1.5 %copy.11 = bf16[4,4,2048]{2,1,0:T(4,128)(2,1)} copy(bf16[4,4,2048]{2,1,0:T(4,128)(2,1)} %shard_map.91) | data formatting | bytes 131072

commit v4 on v3

--- a/solution.py
+++ b/solution.py
@@ -360,7 +360,7 @@
     hbm = pl.BlockSpec(memory_space=pltpu.HBM)
     vmem = pl.BlockSpec(memory_space=pltpu.VMEM)
     dma = pltpu.SemaphoreType.DMA
-    return pl.pallas_call(
+    call = pl.pallas_call(
         functools.partial(body, sizes),
         out_shape=jax.ShapeDtypeStruct((cx, cy, merged), BF16),
         in_specs=[hbm] * 9,
@@ -393,9 +393,10 @@
             dma((ngx,)),
         ],
         compiler_params=pltpu.CompilerParams(
-            collective_id=0, has_side_effects=True, vmem_limit_bytes=60 << 20
+            collective_id=0, has_side_effects=True, vmem_limit_bytes=52 << 20
         ),
-    )(
+    )
+    arrays = (
         volume,
         fine_kernel,
         fine_bias.reshape(1, -1),
@@ -406,6 +407,7 @@
         up_kernel.reshape(ngx, cb, -1),
         up_bias.reshape(1, -1),
     )
+    return call(*(pltpu.with_memory_space_constraint(a, pltpu.HBM) for a in arrays))
 
 
 def solution(mesh):

time: 29.9 us -> 28.4 us (0.950)
  local copies, waits for them, and re-layouts: 1.49 us -> 0.63 us
  Pallas kernels: 28.2 us -> 27.6 us
    unnamed x1, local copies, waits for them, and re-layouts: 1.49 us -> 0.63 us
    pallas_call x1, Pallas kernels: 28.2 us -> 27.6 us  [local(): call(*(pltpu.with_memory_space_constraint(a, pltpu.HBM) for a in arrays))]
where the time goes in v4:
time: 28.4 us; the launch traced here: 28.3 us
  Pallas kernels  27.6 us (97%)
  local copies, waits for them, and re-layouts  0.63 us (2%)
    pallas_call x1, Pallas kernels, local(): call(*(pltpu.with_memory_space_constraint(a, pltpu.HBM) for a in arrays))  27.6 us
    unnamed x1, local copies, waits for them, and re-layouts  0.63 us

profile of v4, /device:TPU:1, one launch (start us, length us, event | category | flops | bytes accessed | tf_op | source)
XLA Modules:
  0.0 28.3 jit_solution(1252659642907273003)
XLA Ops:
  0.0 27.6 %shard_map.91 = bf16[4,4,2048]{2,1,0:T(4,128)(2,1)S(1)} custom-call(bf16[4,4,2048]{2,1,0:T(4,128)(2,1)} %vol_hbm.1, bf16[27,64,64]{2,1,0:T(8,128)(2,1)} %fk_hbm.1, f32[1,64]{1,0:T(1,128)} %bitcast.8, bf16[512,512]{1,0:T(8,128)(2,1)} %dk_hbm.1, f32[1,512]{1,0:T(1,128)} %bitcast.6, bf16[27,512,256]{2,1,0:T(8,128)(2,1)} %bk_hbm.1, f32[1,256]{1,0:T(1,128)} %bitcast.7, ...), custom_call_target="tpu_custom_call" | custom-call | tf_op jit(solution)/shard_map/pallas_call | solution.py:410
  27.6 0.6 %copy.11 = bf16[4,4,2048]{2,1,0:T(4,128)(2,1)} copy(bf16[4,4,2048]{2,1,0:T(4,128)(2,1)S(1)} %shard_map.91) | data formatting | bytes 131072

commit v5 on v4

--- a/solution.py
+++ b/solution.py
@@ -238,12 +238,12 @@
             pl.when(valid(g, other))(getattr(rim(at, b, sending), action))
 
     def others(visit):
-        for d in range(1, ngx):
+        for d in range(ngx - 1, 0, -1):
             for p in (g + d, g - d):
                 pl.when(valid(p, q))(functools.partial(visit, p))
 
+    rims(g, True, "start")
     others(lambda p: block(g, p).start())
-    rims(g, True, "start")
     acc[...] = jnp.zeros_like(acc)
     for load in loads[5:]:
         load.wait()

time: 28.4 us -> 28.7 us (1.011)
  Pallas kernels: 27.6 us -> 27.9 us
    pallas_call x1, Pallas kernels: 27.6 us -> 27.9 us  [local(): call(*(pltpu.with_memory_space_constraint(a, pltpu.HBM) for a in arrays))]
where the time goes in v5:
time: 28.7 us; the launch traced here: 28.6 us
  Pallas kernels  27.9 us (97%)
  local copies, waits for them, and re-layouts  0.63 us (2%)
    pallas_call x1, Pallas kernels, local(): call(*(pltpu.with_memory_space_constraint(a, pltpu.HBM) for a in arrays))  27.9 us
    unnamed x1, local copies, waits for them, and re-layouts  0.63 us

profile of v5, /device:TPU:1, one launch (start us, length us, event | category | flops | bytes accessed | tf_op | source)
XLA Modules:
  0.0 28.6 jit_solution(8711295085660581901)
XLA Ops:
  0.0 27.9 %shard_map.91 = bf16[4,4,2048]{2,1,0:T(4,128)(2,1)S(1)} custom-call(bf16[4,4,2048]{2,1,0:T(4,128)(2,1)} %vol_hbm.1, bf16[27,64,64]{2,1,0:T(8,128)(2,1)} %fk_hbm.1, f32[1,64]{1,0:T(1,128)} %bitcast.8, bf16[512,512]{1,0:T(8,128)(2,1)} %dk_hbm.1, f32[1,512]{1,0:T(1,128)} %bitcast.6, bf16[27,512,256]{2,1,0:T(8,128)(2,1)} %bk_hbm.1, f32[1,256]{1,0:T(1,128)} %bitcast.7, ...), custom_call_target="tpu_custom_call" | custom-call | tf_op jit(solution)/shard_map/pallas_call | solution.py:410
  28.0 0.6 %copy.11 = bf16[4,4,2048]{2,1,0:T(4,128)(2,1)} copy(bf16[4,4,2048]{2,1,0:T(4,128)(2,1)S(1)} %shard_map.91) | data formatting | bytes 131072
